TPU v7x, 32 devices: a whole 2x2x4 slice. The times are simulated.
32 devices in a mesh: parts: 2 (over y), seq: 4 (over z), head: 4 (over x, core).
Axes of the slice: x: 2, y: 2, z: 4, core: 2. Of those that a mesh axis runs over, the one named last changes fastest.
Arguments:
- hidden: bfloat16 [48, 12288], P(('parts', 'head'), 'seq'), parts along dimension 0, may hold values from -600 to 600
- norm_gain: float32 [12288], P('seq'), may hold values from 0.1 to 1.9
- w_query: bfloat16 [12288, 12288], P('seq', 'head'), may hold values from -0.0546875 to 0.0546875
- w_key: bfloat16 [12288, 1024], P('seq', 'head'), may hold values from -0.0546875 to 0.0546875
- w_value: bfloat16 [12288, 1024], P('seq', 'head'), may hold values from -0.0546875 to 0.0546875
- w_out: bfloat16 [12288, 12288], P('head', 'seq'), may hold values from -0.0546875 to 0.0546875
- lengths: int32 [48], P('parts'), parts along dimension 0, may hold values from 1 to 512, as said below
- key_cache: bfloat16 [48, 8, 512, 128], P('parts', 'head', 'seq'), parts along dimension 0, may hold values from -600 to 600, as said below
- value_cache: bfloat16 [48, 8, 512, 128], P('parts', 'head', 'seq'), parts along dimension 0, may hold values from -6 to 6
Outputs:
- attn_out: bfloat16 [48, 12288], P(('parts', 'head'), 'seq'), parts along dimension 0
There are 2 independent parts, one for each index of `parts`. A program takes and returns all parts, laid end to end along the dimension named above; an argument that names none is the same for every part. Nothing has to cross between parts.
Inputs may be any that keep to these rules, and one draw needn't show every extreme that they name: Sequence b holds lengths[b] cached tokens at positions 0 to lengths[b] - 1; its new token takes position lengths[b]. `key_cache`: positions at or past a sequence's length hold no data.
All inputs are finite; a program needn't handle non-finite values.
Results may differ from a plain program's by a relative error of at most 0.0075.
The roundings to bfloat16 on the way count: a program that leaves them out, or rounds other values in their place, can miss the bound.
Values may be sent and summed in bfloat16 or wider, within the bound.
A program may use at most 128 MiB of HBM per device.

v0:
```python
import jax
import jax.numpy as jnp
from jax import lax
from jax.sharding import PartitionSpec as P

D = 12288
EPSILON = 1e-05


def joined(value, axis, join):
    pieces = jax.tree.map(lambda part: lax.all_gather(part, axis), value)
    head = jax.tree.map(lambda part: part[0], pieces)
    tail = jax.tree.map(lambda part: part[1:], pieces)
    subtotal, _ = lax.scan(lambda subtotal, slab: (join(subtotal, slab), None), head, tail)
    return subtotal


def join_parts(earlier, later):
    new_max = jnp.maximum(earlier[0], later[0])
    left_factor = jnp.exp(earlier[0] - new_max)
    right_factor = jnp.exp(later[0] - new_max)
    den_total = earlier[1] * left_factor + later[1] * right_factor
    acc_total = earlier[2] * left_factor[..., None] + later[2] * right_factor[..., None]
    return (new_max, den_total, acc_total)


def local(hidden, norm_gain, w_query, w_key, w_value, w_out, lengths, key_cache, value_cache):
    batch_size, kv_local, block_len, head_size = key_cache.shape
    group_size = w_query.shape[1] // (kv_local * head_size)
    token_rows = lax.all_gather(hidden, "head", axis=0, tiled=True)
    widened = token_rows.astype(jnp.float32)
    square_local = jnp.sum(widened * widened, axis=1)
    scaled = (widened * norm_gain).astype(jnp.bfloat16)
    query_part = jnp.dot(scaled, w_query, preferred_element_type=jnp.float32)
    key_part = jnp.dot(scaled, w_key, preferred_element_type=jnp.float32)
    value_part = jnp.dot(scaled, w_value, preferred_element_type=jnp.float32)
    query_factor = float(head_size) ** (-0.5)
    norm_total = lax.psum(square_local, "seq")
    query_sum, key_sum, value_sum = lax.psum((query_part, key_part, value_part), "seq")
    inverse_rms = lax.rsqrt(norm_total / D + EPSILON)[:, None]
    queries = (query_sum * inverse_rms * query_factor).astype(jnp.bfloat16)
    new_keys = (key_sum * inverse_rms).astype(jnp.bfloat16)
    new_values = (value_sum * inverse_rms).astype(jnp.bfloat16)
    grouped = queries.reshape(batch_size, kv_local, group_size, head_size)
    scores = jnp.einsum("bkgd,bkpd->bkgp", grouped, key_cache, preferred_element_type=jnp.float32)
    offset = lax.axis_index("seq") * block_len
    positions = offset + jnp.arange(block_len, dtype=jnp.int32)
    live_mask = (positions[None, :] < lengths[:, None])[:, None, None, :]
    block_max = jnp.max(jnp.where(live_mask, scores, -1e30), axis=-1)
    shifted = jnp.where(live_mask, scores - block_max[..., None], 0.0)
    weights = jnp.where(live_mask, jnp.exp(shifted), 0.0).astype(jnp.bfloat16)
    block_den = jnp.sum(weights.astype(jnp.float32), axis=-1)
    block_acc = jnp.einsum(
        "bkgp,bkpd->bkgd", weights, value_cache, preferred_element_type=jnp.float32
    )
    self_score = jnp.einsum(
        "oips,ois->oip",
        grouped,
        new_keys.reshape(batch_size, kv_local, head_size),
        preferred_element_type=jnp.float32,
    )
    global_max, den_merged, acc_merged = joined(
        (block_max, block_den, block_acc), "seq", join_parts
    )
    top_score = jnp.maximum(global_max, self_score)
    factors = jnp.exp(global_max - top_score)
    den_sum = den_merged * factors
    acc_sum = acc_merged * factors[..., None]
    own_weight = jnp.exp(self_score - top_score)
    denominator = den_sum + own_weight
    numerator = acc_sum + own_weight[..., None] * new_values.reshape(
        batch_size, kv_local, 1, head_size
    ).astype(jnp.float32)
    mixed = (
        (numerator / denominator[..., None])
        .astype(jnp.bfloat16)
        .reshape(batch_size, kv_local * group_size * head_size)
    )
    output = lax.psum_scatter(
        jnp.dot(mixed, w_out, preferred_element_type=jnp.float32),
        "head",
        scatter_dimension=0,
        tiled=True,
    )
    return output.astype(jnp.bfloat16)


def solution(mesh):
    return jax.shard_map(
        local,
        mesh=mesh,
        in_specs=(
            P(("parts", "head"), "seq"),
            P("seq"),
            P("seq", "head"),
            P("seq", "head"),
            P("seq", "head"),
            P("head", "seq"),
            P("parts"),
            P("parts", "head", "seq", None),
            P("parts", "head", "seq", None),
        ),
        out_specs=P(("parts", "head"), "seq"),
        check_vma=False,
    )
```

profile of v0, /device:TPU:1, one launch (start us, length us, event | category | flops | bytes accessed | tf_op | source)
XLA Modules:
  0.0 132.5 jit_solution(6576906076258920298)
XLA Ops:
  6.5 0.0 copy-start
  6.5 0.0 all-reduce.5.cloned.1.call-start
  6.5 7.0 %all-gather.3 = bf16[4,6,3072]{2,1,0:T(8,128)(2,1)S(1)} all-gather(bf16[1,6,3072]{2,1,0:T(8,128)(2,1)} %bitcast.49), channel_id=1, replica_groups=mesh['parts'=2,'seq'=4,'head'=4] {'head'}, dimensions={0}, use_global_device_ids=true | all-gather | bytes 184320 | tf_op jit(solution)/shard_map/all_gather | solution.py:30
  13.6 0.9 multiply_reduce_fusion
  14.5 0.0 copy-start.1
  14.5 9.8 %fusion.12 = f32[24,3072]{1,0:T(8,128)} fusion(bf16[24,3072]{1,0:T(8,128)(2,1)S(1)} %get-tuple-element.86, bf16[3072,3072]{1,0:T(8,128)(2,1)} %param.13), kind=kOutput, calls=%fused_computation.30 | convolution fusion | flops 452984832 | bytes 19316736 | tf_op jit(solution)/shard_map/dot_general | solution.py:34
  24.3 0.0 all-reduce.5.cloned.1.call-update
  24.3 0.0 all-gather.6.cloned.1.call-start
  24.3 0.0 copy-done.1
  24.3 0.0 copy-start.2
  24.4 0.0 copy-start.4
  24.4 0.3 fusion.15
  24.7 1.1 copy-done.2
  25.8 0.3 fusion.13
  26.1 17.1 %all-reduce.2 = (f32[24]{0:T(128)S(1)}, f32[24,256]{1,0:T(8,128)S(1)}, f32[24,256]{1,0:T(8,128)S(1)}) all-reduce(f32[24]{0:T(128)S(1)} %get-tuple-element.85, f32[24,256]{1,0:T(8,128)S(1)} %fusion.13, f32[24,256]{1,0:T(8,128)S(1)} %fusion.15), channel_id=1, replica_groups=mesh['parts'=2,'seq'=4,'head'=4] {'seq'}, use_global_device_ids=true, to_apply=%region_2.0 | all-reduce | flops 12312 | bytes 98496 | tf_op jit(solution)/shard_map/psum | solution.py:38
  43.2 0.0 copy-done.4
  43.2 0.1 broadcast_compare_fusion
  43.3 16.5 %all-reduce.5.cloned.1.call-done = f32[24,3072]{1,0:T(8,128)} async-done(((f32[24,3072]{1,0:T(8,128)}), f32[24,3072]{1,0:T(8,128)}) %all-reduce.5.cloned.1.call-update) | async-done | bytes 294928 | tf_op jit(solution)/shard_map/psum | solution.py:39
  59.8 1.1 multiply_convert_fusion
  60.8 0.1 reshape.54
  61.0 0.0 copy-done
  61.0 1.0 select_reduce_fusion
  62.0 2.0 %fusion.8 = f32[24,2,12,128]{3,2,1,0:T(8,128)S(1)} fusion(bf16[24,2,128,128]{3,2,1,0:T(8,128)(2,1)} %param.19, f32[24,2,12,128]{3,2,1,0:T(8,128)S(1)} %get-tuple-element.90, f32[24,2,12]{2,1,0:T(2,128)S(1)} %get-tuple-element.89, pred[24,128]{1,0:T(8,128)(4,1)S(1)} %broadcast_compare_fusion), kind=kOutput, calls=%fused_computation.29 | convolution fusion | flops 19169280 | bytes 2168064 | tf_op jit(solution)/shard_map/bkgp,bkpd->bkgd/dot_general | solution.py:53
  64.0 0.9 copy.26
  64.9 0.0 all-gather.6.cloned.1.call-update
  64.9 0.1 fusion.7
  65.0 10.4 %all-gather = f32[96,2,12]{2,1,0:T(2,128)S(1)} all-gather(f32[24,2,12]{2,1,0:T(2,128)S(1)} %get-tuple-element.89), channel_id=2, replica_groups=mesh['parts'=2,'seq'=4,'head'=4] {'seq'}, dimensions={0}, use_global_device_ids=true | all-gather | bytes 11520 | tf_op jit(solution)/shard_map/all_gather | solution.py:11
  75.4 0.4 convert_reduce_fusion
  75.8 11.5 %all-gather.1 = f32[96,2,12]{2,1,0:T(2,128)S(1)} all-gather(f32[24,2,12]{2,1,0:T(2,128)S(1)} %convert_reduce_fusion), channel_id=3, replica_groups=mesh['parts'=2,'seq'=4,'head'=4] {'seq'}, dimensions={0}, use_global_device_ids=true | all-gather | bytes 11520 | tf_op jit(solution)/shard_map/all_gather | solution.py:11
  87.3 0.2 fusion.14
  87.5 0.1 copy.39
  87.6 0.1 copy.29
  87.7 0.1 copy.32
  87.8 0.1 copy.30
  87.9 0.1 copy.33
  88.0 10.4 %all-gather.6.cloned.1.call-done = f32[96,2,12,128]{3,1,2,0:T(2,128)} async-done(((f32[24,2,12,128]{3,1,2,0:T(2,128)}), f32[96,2,12,128]{3,1,2,0:T(2,128)}) %all-gather.6.cloned.1.call-update) | async-done | bytes 1179664 | tf_op jit(solution)/shard_map/all_gather | solution.py:11
  98.5 0.0 slice-start
  98.5 1.1 slice.32
  99.6 0.1 slice-done
  99.7 2.0 %while.14 = (s32[]{:T(128)}, f32[24,2,12]{0,1,2:T(2,128)S(1)}, f32[24,2,12]{0,1,2:T(2,128)S(1)}, f32[24,2,12,128]{3,2,1,0:T(8,128)S(1)}, f32[3,24,2,12]{1,2,3,0:...) while((s32[]{:T(128)}, f32[24,2,12]{0,1,2:T(2,128)S(1)}, ...), condition=%wide.region_6.7_spmd, body=%wide.region_5.6_spmd.sunk | while | flops 224642 | bytes 1506917 | solution.py:14
  99.8 0.1 copy.54
  99.9 0.1 copy.55
  100.0 0.4 fusion.33
  100.4 0.1 copy.54
  100.5 0.1 copy.55
  100.7 0.4 fusion.33
  101.1 0.1 copy.54
  101.2 0.1 copy.55
  101.3 0.4 fusion.33
  101.7 0.1 copy.37
  101.8 0.1 copy.35
  101.9 0.1 copy.36
  102.0 0.4 divide_convert_fusion
  102.4 0.1 reshape.56
  102.5 0.0 copy-start.3
  102.5 7.7 %fusion.16 = f32[24,3072]{1,0:T(8,128)S(1)} fusion(bf16[24,3072]{1,0:T(8,128)(2,1)S(1)} %reshape.56, bf16[3072,3072]{1,0:T(8,128)(2,1)} %param.16), kind=kOutput, calls=%fused_computation.34 | convolution fusion | flops 452984832 | bytes 19316736 | tf_op jit(solution)/shard_map/dot_general | solution.py:80
  110.2 9.0 %fusion = f32[8,3072]{1,0:T(8,128)S(1)} fusion(f32[24,3072]{1,0:T(8,128)S(1)} %fusion.16), kind=kCustom, calls=%all-reduce-scatter | all-reduce-scatter fusion | flops 98305 | bytes 393728
  119.2 4.3 %collective-permute-start = (bf16[6,3072]{1,0:T(8,128)(2,1)S(1)}, bf16[6,3072]{1,0:T(8,128)(2,1)S(1)}, u32[]{:S(2)}, u32[]{:S(2)}) collective-permute-start(bf16[6,3072]{1,0:T(8,128)(2,1)S(1)} %slice.36), channel_id=1, source_target_pairs={{0,1},{1,2},{2,3},{4,5},{5,6},{6,7},{8,9},{9,10},{10,11},{12,13},{... | collective-permute-start | bytes 110600
  123.6 0.0 copy-done.3
  123.6 0.6 dynamic-slice.4
  124.8 0.0 collective-permute-done
  124.8 0.2 concatenate
  125.0 0.6 dynamic-slice_convert_fusion
  (18 shorter events, 0.4 us)
Async XLA Ops:
  6.5 54.4 %copy-start = (bf16[24,2,128,128]{3,2,1,0:T(8,128)(2,1)S(1)}, bf16[24,2,128,128]{3,2,1,0:T(8,128)(2,1)}, u32[]{:S(2)}) copy-start(bf16[24,2,128,128]{3,2,1,0:T(8,128)(2,1)} %param.18) | copy-start | bytes 4718596
  6.5 53.2 %all-reduce.5.cloned.1.call-start = ((), (), s32[]{:S(2)}) async-start(), calls=%async_computation | async-start | bytes 589824 | tf_op jit(solution)/shard_map/psum | solution.py:39
  14.5 9.8 %copy-start.1 = (bf16[3072,256]{1,0:T(8,128)(2,1)S(1)}, bf16[3072,256]{1,0:T(8,128)(2,1)}, u32[]{:S(2)}) copy-start(bf16[3072,256]{1,0:T(8,128)(2,1)} %param.15) | copy-start | bytes 4718596
  24.3 74.2 %all-gather.6.cloned.1.call-start = ((), (), s32[]{:S(2)}) async-start(), calls=%async_computation.1 | async-start | bytes 1474560 | tf_op jit(solution)/shard_map/all_gather | solution.py:11
  24.3 1.4 %copy-start.2 = (bf16[3072,256]{1,0:T(8,128)(2,1)S(1)}, bf16[3072,256]{1,0:T(8,128)(2,1)}, u32[]{:S(2)}) copy-start(bf16[3072,256]{1,0:T(8,128)(2,1)} %param.14) | copy-start | bytes 4718596
  24.4 18.9 %copy-start.4 = (s32[24]{0:T(128)S(1)}, s32[24]{0:T(128)}, u32[]{:S(2)}) copy-start(s32[24]{0:T(128)} %param.17) | copy-start | bytes 292
  98.5 1.3 slice-start
  102.5 21.0 %copy-start.3 = (u32[32]{0:T(128)S(1)}, u32[32]{0:T(128)}, u32[]{:S(2)}) copy-start(u32[32]{0:T(128)} %constant.37) | copy-start | bytes 388
  119.2 5.6 %collective-permute-start = (bf16[6,3072]{1,0:T(8,128)(2,1)S(1)}, bf16[6,3072]{1,0:T(8,128)(2,1)S(1)}, u32[]{:S(2)}, u32[]{:S(2)}) collective-permute-start(bf16[6,3072]{1,0:T(8,128)(2,1)S(1)} %slice.36), channel_id=1, source_target_pairs={{0,1},{1,2},{2,3},{4,5},{5,6},{6,7},{8,9},{9,10},{10,11},{12,13},{... | collective-permute-start | bytes 110600
Sparse Core Ops, SparseCore 0:
  24.4 35.3 all-reduce.4
  65.0 33.4 all-gather.5
where the time goes:
time: 133 us; the launch traced here: 132 us
  blocking collectives  55.1 us (41%)
  waiting for transfers between devices  26.9 us (20%)
  matrix products  21.3 us (16%)
  between operations  14.3 us (11%)
  local copies, waits for them, and re-layouts  6.41 us (5%)
  starting transfers between devices  4.35 us (3%)
  other arithmetic  4.09 us (3%)
    all_gather x2, blocking collectives, joined(): pieces = jax.tree.map(lambda part: lax.all_gather(part, axis), value)  21.9 us
    psum x1, blocking collectives, local(): norm_total = lax.psum(square_local, 'seq')  17.1 us
    psum x1, waiting for transfers between devices, local(): lax.psum((query_part, key_part, value_part), 'seq')  16.5 us
    all_gather x1, waiting for transfers between devices, joined(): pieces = jax.tree.map(lambda part: lax.all_gather(part, axis), value)  10.4 us
    dot_general x1, matrix products, local(): query_part = jnp.dot(scaled, w_query, preferred_element_type=jnp.float32)  9.76 us
    unnamed x1, blocking collectives  8.98 us
    dot_general x1, matrix products, local(): jnp.dot(mixed, w_out, preferred_element_type=jnp.float32)  7.7 us
    all_gather x1, blocking collectives, local(): token_rows = lax.all_gather(hidden, 'head', axis=0, tiled=True)  7.05 us
  transfers between devices with their start and end apart: 3, of which 2 were waited for; matrix products, arithmetic and copies ran while one was open for 2% of the time, Pallas kernels for 0%

commit v1 on v0

--- a/solution.py
+++ b/solution.py
@@ -35,7 +35,7 @@
     key_part = jnp.dot(scaled, w_key, preferred_element_type=jnp.float32)
     value_part = jnp.dot(scaled, w_value, preferred_element_type=jnp.float32)
     query_factor = float(head_size) ** (-0.5)
-    norm_total = lax.psum(square_local, "seq")
+    norm_total = jnp.sum(lax.all_gather(square_local, "seq"), axis=0)
     query_sum, key_sum, value_sum = lax.psum((query_part, key_part, value_part), "seq")
     inverse_rms = lax.rsqrt(norm_total / D + EPSILON)[:, None]
     queries = (query_sum * inverse_rms * query_factor).astype(jnp.bfloat16)

time: 133 us -> 133 us (level)
    psum x1 -> x0, blocking collectives: 17.1 us -> none  [local(): norm_total = lax.psum(square_local, 'seq')]
    unnamed x1 -> x2, blocking collectives: 8.98 us -> 25.5 us
    unnamed x13 -> x18, local copies, waits for them, and re-layouts: 1.86 us -> 2.69 us
  transfers between devices with their start and end apart: 3 -> 3, of which waited for: 2 -> 2; matrix products, arithmetic and copies ran while one was open for 2% -> 3% of each run, Pallas kernels for 0% -> 0%
where the time goes in v1:
time: 133 us; the launch traced here: 132 us
  blocking collectives  54.4 us (41%)
  waiting for transfers between devices  25.8 us (19%)
  matrix products  21.3 us (16%)
  between operations  14.9 us (11%)
  local copies, waits for them, and re-layouts  7.32 us (6%)
  starting transfers between devices  4.35 us (3%)
  other arithmetic  4.11 us (3%)
    unnamed x2, blocking collectives  25.5 us
    all_gather x2, blocking collectives, joined(): pieces = jax.tree.map(lambda part: lax.all_gather(part, axis), value)  21.9 us
    psum x1, waiting for transfers between devices, local(): lax.psum((query_part, key_part, value_part), 'seq')  15.4 us
    all_gather x1, waiting for transfers between devices, joined(): pieces = jax.tree.map(lambda part: lax.all_gather(part, axis), value)  10.4 us
    dot_general x1, matrix products, local(): query_part = jnp.dot(scaled, w_query, preferred_element_type=jnp.float32)  9.75 us
    dot_general x1, matrix products, local(): jnp.dot(mixed, w_out, preferred_element_type=jnp.float32)  7.7 us
    all_gather x1, blocking collectives, local(): token_rows = lax.all_gather(hidden, 'head', axis=0, tiled=True)  7.05 us
    unnamed x1, starting transfers between devices  4.3 us
  transfers between devices with their start and end apart: 3, of which 2 were waited for; matrix products, arithmetic and copies ran while one was open for 3% of the time, Pallas kernels for 0%

profile of v1, /device:TPU:1, one launch (start us, length us, event | category | flops | bytes accessed | tf_op | source)
XLA Modules:
  0.0 132.4 jit_solution(15266003411170719758)
XLA Ops:
  6.5 0.0 copy-start
  6.5 0.0 all-reduce.6.cloned.1.call-start
  6.5 7.0 %all-gather.4 = bf16[4,6,3072]{2,1,0:T(8,128)(2,1)S(1)} all-gather(bf16[1,6,3072]{2,1,0:T(8,128)(2,1)} %bitcast.50), channel_id=1, replica_groups=mesh['parts'=2,'seq'=4,'head'=4] {'head'}, dimensions={0}, use_global_device_ids=true | all-gather | bytes 184320 | tf_op jit(solution)/shard_map/all_gather | solution.py:30
  13.6 0.9 multiply_reduce_fusion
  14.5 9.8 %fusion.12 = f32[24,3072]{1,0:T(8,128)} fusion(bf16[24,3072]{1,0:T(8,128)(2,1)S(1)} %get-tuple-element.86, bf16[3072,3072]{1,0:T(8,128)(2,1)} %param.13), kind=kOutput, calls=%fused_computation.30 | convolution fusion | flops 452984832 | bytes 19316736 | tf_op jit(solution)/shard_map/dot_general | solution.py:34
  24.2 0.0 all-reduce.6.cloned.1.call-update
  24.3 0.0 all-gather.7.cloned.1.call-start
  24.3 0.0 copy-done.1
  24.3 0.0 copy-start.2
  24.3 0.0 copy-start.5
  24.4 0.0 copy-start.4
  24.4 0.3 fusion.15
  24.7 1.1 copy-done.2
  25.7 0.3 fusion.13
  26.1 0.0 copy-done.5
  26.1 0.6 dynamic-slice
  27.3 0.2 dynamic-update-slice
  27.6 16.5 %all-reduce.3 = (f32[96]{0:T(128)S(1)}, f32[24,256]{1,0:T(8,128)S(1)}, f32[24,256]{1,0:T(8,128)S(1)}) all-reduce(f32[96]{0:T(128)S(1)} %dynamic-update-slice, f32[24,256]{1,0:T(8,128)S(1)} %fusion.13, f32[24,256]{1,0:T(8,128)S(1)} %fusion.15), channel_id=2, replica_groups=mesh['parts'=2,'seq'=4,'head'=4] {'seq'}, use_global_device_ids=true, to_apply=%add | all-reduce | flops 12384 | bytes 99072
  44.1 0.1 reshape.62
  44.2 0.0 copy-done.4
  44.2 0.1 broadcast_compare_fusion
  44.3 15.4 %all-reduce.6.cloned.1.call-done = f32[24,3072]{1,0:T(8,128)} async-done(((f32[24,3072]{1,0:T(8,128)}), f32[24,3072]{1,0:T(8,128)}) %all-reduce.6.cloned.1.call-update) | async-done | bytes 294928 | tf_op jit(solution)/shard_map/psum | solution.py:39
  59.7 1.1 multiply_convert_fusion
  60.7 0.1 reshape.58
  60.8 1.0 select_reduce_fusion
  61.8 2.0 %fusion.8 = f32[24,2,12,128]{3,2,1,0:T(8,128)S(1)} fusion(bf16[24,2,128,128]{3,2,1,0:T(8,128)(2,1)} %param.19, f32[24,2,12,128]{3,2,1,0:T(8,128)S(1)} %get-tuple-element.90, f32[24,2,12]{2,1,0:T(2,128)S(1)} %get-tuple-element.89, pred[24,128]{1,0:T(8,128)(4,1)S(1)} %broadcast_compare_fusion), kind=kOutput, calls=%fused_computation.29 | convolution fusion | flops 19169280 | bytes 2168064 | tf_op jit(solution)/shard_map/bkgp,bkpd->bkgd/dot_general | solution.py:53
  63.9 0.9 copy.26
  64.7 0.0 all-gather.7.cloned.1.call-update
  64.8 0.1 fusion.7
  64.9 10.4 %all-gather.1 = f32[96,2,12]{2,1,0:T(2,128)S(1)} all-gather(f32[24,2,12]{2,1,0:T(2,128)S(1)} %get-tuple-element.89), channel_id=3, replica_groups=mesh['parts'=2,'seq'=4,'head'=4] {'seq'}, dimensions={0}, use_global_device_ids=true | all-gather | bytes 11520 | tf_op jit(solution)/shard_map/all_gather | solution.py:11
  75.3 0.4 convert_reduce_fusion
  75.6 11.5 %all-gather.2 = f32[96,2,12]{2,1,0:T(2,128)S(1)} all-gather(f32[24,2,12]{2,1,0:T(2,128)S(1)} %convert_reduce_fusion), channel_id=4, replica_groups=mesh['parts'=2,'seq'=4,'head'=4] {'seq'}, dimensions={0}, use_global_device_ids=true | all-gather | bytes 11520 | tf_op jit(solution)/shard_map/all_gather | solution.py:11
  87.2 0.2 fusion.14
  87.4 0.1 copy.39
  87.5 0.1 copy.29
  87.6 0.1 copy.32
  87.7 0.1 copy.30
  87.8 0.1 copy.33
  87.9 10.4 %all-gather.7.cloned.1.call-done = f32[96,2,12,128]{3,1,2,0:T(2,128)} async-done(((f32[24,2,12,128]{3,1,2,0:T(2,128)}), f32[96,2,12,128]{3,1,2,0:T(2,128)}) %all-gather.7.cloned.1.call-update) | async-done | bytes 1179664 | tf_op jit(solution)/shard_map/all_gather | solution.py:11
  98.4 1.1 slice.32
  99.5 0.1 slice-done
  99.6 2.0 %while.14 = (s32[]{:T(128)}, f32[24,2,12]{0,1,2:T(2,128)S(1)}, f32[24,2,12]{0,1,2:T(2,128)S(1)}, f32[24,2,12,128]{3,2,1,0:T(8,128)S(1)}, f32[3,24,2,12]{1,2,3,0:...) while((s32[]{:T(128)}, f32[24,2,12]{0,1,2:T(2,128)S(1)}, ...), condition=%wide.region_6.7_spmd, body=%wide.region_5.6_spmd.sunk | while | flops 224642 | bytes 1506917 | solution.py:14
  99.7 0.1 copy.54
  99.8 0.1 copy.55
  99.9 0.4 fusion.33
  100.3 0.1 copy.54
  100.4 0.1 copy.55
  100.5 0.4 fusion.33
  101.0 0.1 copy.54
  101.1 0.1 copy.55
  101.2 0.4 fusion.33
  101.6 0.1 copy.37
  101.7 0.1 copy.35
  101.8 0.1 copy.36
  101.9 0.4 divide_convert_fusion
  102.3 0.1 reshape.60
  102.4 0.0 copy-start.3
  102.4 7.7 %fusion.16 = f32[24,3072]{1,0:T(8,128)S(1)} fusion(bf16[24,3072]{1,0:T(8,128)(2,1)S(1)} %reshape.60, bf16[3072,3072]{1,0:T(8,128)(2,1)} %param.16), kind=kOutput, calls=%fused_computation.34 | convolution fusion | flops 452984832 | bytes 19316736 | tf_op jit(solution)/shard_map/dot_general | solution.py:80
  110.1 9.0 %fusion = f32[8,3072]{1,0:T(8,128)S(1)} fusion(f32[24,3072]{1,0:T(8,128)S(1)} %fusion.16), kind=kCustom, calls=%all-reduce-scatter | all-reduce-scatter fusion | flops 98305 | bytes 393728
  119.1 4.3 %collective-permute-start = (bf16[6,3072]{1,0:T(8,128)(2,1)S(1)}, bf16[6,3072]{1,0:T(8,128)(2,1)S(1)}, u32[]{:S(2)}, u32[]{:S(2)}) collective-permute-start(bf16[6,3072]{1,0:T(8,128)(2,1)S(1)} %slice.36), channel_id=1, source_target_pairs={{0,1},{1,2},{2,3},{4,5},{5,6},{6,7},{8,9},{9,10},{10,11},{12,13},{... | collective-permute-start | bytes 110600
  123.5 0.6 dynamic-slice.5
  124.7 0.0 collective-permute-done
  124.7 0.2 concatenate
  124.9 0.6 dynamic-slice_convert_fusion
  (24 shorter events, 0.4 us)
Async XLA Ops:
  6.5 54.3 %copy-start = (bf16[24,2,128,128]{3,2,1,0:T(8,128)(2,1)S(1)}, bf16[24,2,128,128]{3,2,1,0:T(8,128)(2,1)}, u32[]{:S(2)}) copy-start(bf16[24,2,128,128]{3,2,1,0:T(8,128)(2,1)} %param.18) | copy-start | bytes 4718596
  6.5 53.1 %all-reduce.6.cloned.1.call-start = ((), (), s32[]{:S(2)}) async-start(), calls=%async_computation | async-start | bytes 589824 | tf_op jit(solution)/shard_map/psum | solution.py:39
  14.5 9.8 %copy-start.1 = (bf16[3072,256]{1,0:T(8,128)(2,1)S(1)}, bf16[3072,256]{1,0:T(8,128)(2,1)}, u32[]{:S(2)}) copy-start(bf16[3072,256]{1,0:T(8,128)(2,1)} %param.15) | copy-start | bytes 4718596
  24.3 74.1 %all-gather.7.cloned.1.call-start = ((), (), s32[]{:S(2)}) async-start(), calls=%async_computation.1 | async-start | bytes 1474560 | tf_op jit(solution)/shard_map/all_gather | solution.py:11
  24.3 1.4 %copy-start.2 = (bf16[3072,256]{1,0:T(8,128)(2,1)S(1)}, bf16[3072,256]{1,0:T(8,128)(2,1)}, u32[]{:S(2)}) copy-start(bf16[3072,256]{1,0:T(8,128)(2,1)} %param.14) | copy-start | bytes 4718596
  24.3 1.7 %copy-start.5 = (u32[32]{0:T(128)S(1)}, u32[32]{0:T(128)}, u32[]{:S(2)}) copy-start(u32[32]{0:T(128)} %constant.37) | copy-start | bytes 388
  24.4 19.8 %copy-start.4 = (s32[24]{0:T(128)S(1)}, s32[24]{0:T(128)}, u32[]{:S(2)}) copy-start(s32[24]{0:T(128)} %param.17) | copy-start | bytes 292
  98.4 1.3 slice-start
  102.4 21.0 %copy-start.3 = (u32[32]{0:T(128)S(1)}, u32[32]{0:T(128)}, u32[]{:S(2)}) copy-start(u32[32]{0:T(128)} %constant.43) | copy-start | bytes 388
  119.1 5.6 %collective-permute-start = (bf16[6,3072]{1,0:T(8,128)(2,1)S(1)}, bf16[6,3072]{1,0:T(8,128)(2,1)S(1)}, u32[]{:S(2)}, u32[]{:S(2)}) collective-permute-start(bf16[6,3072]{1,0:T(8,128)(2,1)S(1)} %slice.36), channel_id=1, source_target_pairs={{0,1},{1,2},{2,3},{4,5},{5,6},{6,7},{8,9},{9,10},{10,11},{12,13},{... | collective-permute-start | bytes 110600
Sparse Core Ops, SparseCore 0:
  24.4 35.2 all-reduce.5
  64.9 33.4 all-gather.6
